TPU v7x, 128 devices: a whole 4x4x4 slice. The times are simulated.
128 devices in a mesh: row: 16 (over x, z), col: 8 (over y, core).
Axes of the slice: x: 4, y: 4, z: 4, core: 2. Of those that a mesh axis runs over, the one named last changes fastest.
Arguments:
- tokens: bfloat16 [384, 8192], P('col', 'row'), may hold values from -6 to 6
- gate_weight: bfloat16 [8192, 26624], P('row', 'col'), may hold values from -0.09375 to 0.09375
- up_weight: bfloat16 [8192, 26624], P('row', 'col'), may hold values from -0.09375 to 0.09375
- down_weight: bfloat16 [26624, 8192], P('col', 'row'), may hold values from -0.0546875 to 0.0546875
- gate_mask: int32 [64, 208], P('row', 'col'), may hold values from 0 to 1, as said below
- up_mask: int32 [64, 208], P('row', 'col'), may hold values from 0 to 1, as said below
- down_mask: int32 [208, 64], P('col', 'row'), may hold values from 0 to 1, as said below
- out_grad: bfloat16 [384, 8192], P('col', 'row'), may hold values from -6 to 6
Outputs:
- mixed_out: bfloat16 [384, 8192], P('col', 'row')
- grad_gate: bfloat16 [8192, 26624], P('row', 'col')
- grad_up: bfloat16 [8192, 26624], P('row', 'col')
- grad_down: bfloat16 [26624, 8192], P('col', 'row')
- input_grad: bfloat16 [384, 8192], P('col', 'row')
Inputs may be any that keep to these rules, and one draw needn't show every extreme that they name: `gate_mask`: 1 keeps a tile of 128 x 128 weights, 0 drops it; the share kept differs between rows of tiles. `up_mask`: 1 keeps a tile of 128 x 128 weights, 0 drops it; the share kept differs between rows of tiles. `down_mask`: 1 keeps a tile of 128 x 128 weights, 0 drops it; the share kept differs between columns of tiles.
All inputs are finite; a program needn't handle non-finite values.
Results may differ from a plain program's by a relative error of at most 0.0049.
Values may be sent and summed in bfloat16 or wider, within the bound.
A program may use at most 128 MiB of HBM per device.

v0:
```python
import jax
import jax.numpy as jnp
from jax import lax
from jax.sharding import PartitionSpec as P


def expand(weight, mask):
    rows_w, cols_w = weight.shape
    tile_size = rows_w // mask.shape[0]
    blocks = weight.reshape(mask.shape[0], tile_size, mask.shape[1], tile_size)
    kept = mask.astype(weight.dtype)[:, None, :, None]
    return (blocks * kept).reshape(rows_w, cols_w)


def contract_last(left, right):
    return lax.dot_general(
        left, right, (((1,), (1,)), ((), ())), preferred_element_type=jnp.float32
    )


def contract_first(left, right):
    return lax.dot_general(
        left, right, (((0,), (0,)), ((), ())), preferred_element_type=jnp.float32
    )


def body(tokens, gate_weight, up_weight, down_weight, gate_mask, up_mask, down_mask, out_grad):
    feat = tokens.shape[1]
    both_all = lax.all_gather(
        jnp.concatenate([tokens, out_grad], axis=1), "col", axis=0, tiled=True
    )
    tok_all = both_all[:, :feat]
    grad_all = both_all[:, feat:]
    w_gate = expand(gate_weight, gate_mask)
    w_up = expand(up_weight, up_mask)
    w_down = expand(down_weight, down_mask)
    gate_mine = lax.psum_scatter(
        jnp.dot(tok_all, w_gate, preferred_element_type=jnp.float32),
        "row",
        scatter_dimension=0,
        tiled=True,
    )
    up_mine = lax.psum_scatter(
        jnp.dot(tok_all, w_up, preferred_element_type=jnp.float32),
        "row",
        scatter_dimension=0,
        tiled=True,
    )
    sigmoid_gate = jax.nn.sigmoid(gate_mine)
    silu_gate = gate_mine * sigmoid_gate
    hidden_mine = (silu_gate * up_mine).astype(jnp.bfloat16)
    hidden_all = lax.all_gather(hidden_mine, "row", axis=0, tiled=True)
    hidden_grad = lax.psum_scatter(
        contract_last(grad_all, w_down), "row", scatter_dimension=0, tiled=True
    )
    gate_grad = (
        hidden_grad * up_mine * sigmoid_gate * (1.0 + gate_mine * (1.0 - sigmoid_gate))
    ).astype(jnp.bfloat16)
    up_grad = (hidden_grad * silu_gate).astype(jnp.bfloat16)
    grad_pair = lax.all_gather(
        jnp.concatenate([gate_grad, up_grad], axis=1), "row", axis=0, tiled=True
    )
    half_width = gate_weight.shape[1]
    weight_pair = contract_first(tok_all, grad_pair)
    grad_gate = expand(weight_pair[:, :half_width], gate_mask).astype(jnp.bfloat16)
    grad_up = expand(weight_pair[:, half_width:], up_mask).astype(jnp.bfloat16)
    grad_down = expand(contract_first(hidden_all, grad_all), down_mask).astype(jnp.bfloat16)
    mixed_part = jnp.dot(hidden_all, w_down, preferred_element_type=jnp.float32)
    input_part = contract_last(grad_pair[:, :half_width], w_gate) + contract_last(
        grad_pair[:, half_width:], w_up
    )
    out_sums = lax.psum_scatter(
        jnp.concatenate([mixed_part, input_part], axis=1), "col", scatter_dimension=0, tiled=True
    )
    mixed_out = out_sums[:, :feat].astype(jnp.bfloat16)
    input_grad = out_sums[:, feat:].astype(jnp.bfloat16)
    return (mixed_out, grad_gate, grad_up, grad_down, input_grad)


def solution(mesh):
    in_specs = (
        P("col", "row"),
        P("row", "col"),
        P("row", "col"),
        P("col", "row"),
        P("row", "col"),
        P("row", "col"),
        P("col", "row"),
        P("col", "row"),
    )
    out_specs = (
        P("col", "row"),
        P("row", "col"),
        P("row", "col"),
        P("col", "row"),
        P("col", "row"),
    )
    return jax.shard_map(body, mesh=mesh, in_specs=in_specs, out_specs=out_specs, check_vma=False)
```

profile of v0, /device:TPU:1, one launch (start us, length us, event | category | flops | bytes accessed | tf_op | source)
XLA Modules:
  0.0 446.2 jit_solution(16238817399744067588)
XLA Ops:
  8.0 16.3 %all_gather.9 = bf16[384,1024]{1,0:T(8,128)(2,1)} all-gather(bf16[48,1024]{1,0:T(8,128)(2,1)S(1)} %pad_maximum_fusion.2), channel_id=1, replica_groups=mesh['row'=16,'col'=8] {'col'}, dimensions={0}, use_global_device_ids=true | all-gather | bytes 884736 | tf_op jit(solution)/shard_map/all_gather | solution.py:29
  25.2 4.2 copy.26
  29.5 0.9 mul.87
  30.4 1.7 copy-done
  32.2 3.9 fusion.10
  36.8 5.6 %copy.28 = bf16[512,3328]{0,1:T(8,128)(2,1)} copy(bf16[512,3328]{1,0:T(8,128)(2,1)} %param.10) | data formatting | bytes 6815744 | tf_op args[2]
  42.4 0.9 mul.91
  43.4 1.7 copy-done.3
  45.1 4.9 %fusion.11 = f32[384,3328]{1,0:T(8,128)} fusion(bf16[512,3328]{0,1:T(8,128)(2,1)S(1)} %copy-done.2, bf16[416,8,4,128]{3,2,1,0:T(4,128)(2,1)S(1)} %bitcast.53, bf16[384,1024]{1,0:T(8,128)(2,1)} %all_gather.9), kind=kOutput, calls=%fused_computation.18 | convolution fusion | flops 1310326784 | bytes 12320768 | tf_op jit(solution)/shard_map/dot_general | solution.py:44
  50.8 0.9 mul.95
  51.8 1.7 copy-done.4
  53.5 5.9 %fusion.12 = f32[384,3328]{1,0:T(8,128)} fusion(bf16[3328,512]{1,0:T(8,128)(2,1)} %param.11, bf16[416,8,4,128]{3,2,1,0:T(4,128)(2,1)S(1)} %bitcast.55, bf16[384,1024]{1,0:T(8,128)(2,1)S(1)} %copy-done.6), kind=kOutput, calls=%fused_computation.19 | convolution fusion | flops 1310326784 | bytes 12320768 | tf_op jit(solution)/shard_map/dot_general | solution.py:16
  59.4 56.1 %reduce-scatter.13.cloned.1.call-done = f32[24,3328]{1,0:T(8,128)} async-done(((f32[384,3328]{1,0:T(8,128)}), f32[24,3328]{1,0:T(8,128)}) %reduce-scatter.13.cloned.1.call-update) | async-done | bytes 319504
  115.5 82.6 %reduce-scatter.15.cloned.1.call-done = f32[24,3328]{1,0:T(8,128)} async-done(((f32[384,3328]{1,0:T(8,128)}), f32[24,3328]{1,0:T(8,128)}) %reduce-scatter.15.cloned.1.call-update) | async-done | bytes 319504
  198.1 82.6 %reduce-scatter.17.cloned.1.call-done = f32[24,3328]{1,0:T(8,128)} async-done(((f32[384,3328]{1,0:T(8,128)}), f32[24,3328]{1,0:T(8,128)}) %reduce-scatter.17.cloned.1.call-update) | async-done | bytes 319504
  280.7 2.1 multiply_convert_fusion.2
  282.9 1.8 pad_maximum_fusion.1
  284.9 44.2 %all-gather.3.cloned.1.call-done = bf16[384,3328]{1,0:T(8,128)(2,1)} async-done(((bf16[24,3328]{1,0:T(8,128)(2,1)}), bf16[384,3328]{1,0:T(8,128)(2,1)}) %all-gather.3.cloned.1.call-update) | async-done | bytes 2555920 | tf_op jit(solution)/shard_map/all_gather | solution.py:52
  329.1 6.1 %fusion.13 = f32[384,512]{1,0:T(8,128)} fusion(bf16[384,3328]{1,0:T(8,128)(2,1)} %all-gather.3.cloned.1.call-done, bf16[3328,512]{1,0:T(8,128)(2,1)} %param.11, bf16[416,8,4,128]{3,2,1,0:T(4,128)(2,1)} %bitcast.56), kind=kOutput, calls=%fused_computation.20 | convolution fusion | flops 1310326784 | bytes 10158080 | tf_op jit(solution)/shard_map/dot_general | solution.py:68
  335.2 51.6 %all-gather.5.cloned.1.call-done = bf16[384,6656]{1,0:T(8,128)(2,1)} async-done(((bf16[24,6656]{1,0:T(8,128)(2,1)}), bf16[384,6656]{1,0:T(8,128)(2,1)}) %all-gather.5.cloned.1.call-update) | async-done | bytes 5111824 | tf_op jit(solution)/shard_map/all_gather | solution.py:60
  386.8 5.4 %fusion.3 = f32[384,512]{1,0:T(8,128)S(1)} fusion(bf16[384,6656]{1,0:T(8,128)(2,1)} %all-gather.5.cloned.1.call-done, bf16[512,3328]{0,1:T(8,128)(2,1)} %copy.28, bf16[416,8,4,128]{3,2,1,0:T(4,128)(2,1)} %bitcast.54), kind=kOutput, calls=%fused_computation.11 | convolution fusion | flops 1310326784 | bytes 10158080 | tf_op jit(solution)/shard_map/dot_general | solution.py:16
  393.0 1.5 fusion.7
  394.5 1.4 pad_maximum_fusion
  396.0 0.9 mul.103
  397.0 3.6 copy.54
  400.6 7.7 %copy.31 = f32[512,3328]{1,0:T(8,128)} copy(f32[512,3328]{0,1:T(8,128)} %bitcast.48) | data formatting | bytes 13631488 | tf_op jit(solution)/shard_map/mul | solution.py:12
  408.4 0.9 mul.106
  409.3 3.5 copy.53
  412.8 7.7 %copy.33 = f32[512,3328]{1,0:T(8,128)} copy(f32[512,3328]{0,1:T(8,128)} %bitcast.50) | data formatting | bytes 13631488 | tf_op jit(solution)/shard_map/mul | solution.py:12
  422.6 3.8 fusion
  426.3 3.8 fusion.17
  430.1 7.7 %fusion.1 = (bf16[512,3328]{1,0:T(8,128)(2,1)}, bf16[512,3328]{1,0:T(8,128)(2,1)}) fusion(f32[512,3328]{1,0:T(8,128)} %copy.33, f32[512,6656]{1,0:T(8,128)S(1)} %fusion.17, f32[512,3328]{1,0:T(8,128)} %copy.31), kind=kLoop, calls=%fused_computation.5 | loop fusion | flops 6815744 | bytes 34078720 | tf_op jit(solution)/shard_map/convert_element_type | solution.py:66
  (54 shorter events, 8.4 us)
Async XLA Ops:
  7.2 108.3 %reduce-scatter.13.cloned.1.call-start = ((), (), s32[]{:S(2)}) async-start(), calls=%async_computation.7 | async-start | bytes 5431296
  29.5 2.7 copy-start.5
  30.4 1.8 copy-start
  36.0 0.7 copy-start.11
  36.1 162.0 %reduce-scatter.15.cloned.1.call-start = ((), (), s32[]{:S(2)}) async-start(), calls=%async_computation.8 | async-start | bytes 5431296
  42.4 2.7 copy-start.2
  43.4 1.8 copy-start.3
  50.0 0.7 copy-start.12
  50.0 230.7 %reduce-scatter.17.cloned.1.call-start = ((), (), s32[]{:S(2)}) async-start(), calls=%async_computation.9 | async-start | bytes 5431296
  50.8 2.7 copy-start.6
  51.7 1.7 copy-start.4
  59.4 269.7 %all-gather.3.cloned.1.call-start = ((), (), s32[]{:S(2)}) async-start(), calls=%async_computation.4 | async-start | bytes 2715648 | tf_op jit(solution)/shard_map/all_gather | solution.py:52
  282.8 104.0 %all-gather.5.cloned.1.call-start = ((), (), s32[]{:S(2)}) async-start(), calls=%async_computation.5 | async-start | bytes 5431296 | tf_op jit(solution)/shard_map/all_gather | solution.py:60
  284.7 153.1 %reduce-scatter.11.cloned.1.call-start = ((), (), s32[]{:S(2)}) async-start(), calls=%async_computation.6 | async-start | bytes 1769472 | tf_op jit(solution)/shard_map/reduce_scatter | solution.py:72
  386.8 5.4 %copy-start.1 = (bf16[4,128,26,128]{1,0,3,2:T(4,128)(2,1)S(1)}, bf16[4,128,26,128]{1,0,3,2:T(4,128)(2,1)}, u32[]{:S(2)}) copy-start(bf16[4,128,26,128]{1,0,3,2:T(4,128)(2,1)} %copy-done) | copy-start | bytes 10223620
  386.8 6.2 %copy-start.9 = (bf16[384,6656]{1,0:T(8,128)(2,1)S(1)}, bf16[384,6656]{1,0:T(8,128)(2,1)}, u32[]{:S(2)}) copy-start(bf16[384,6656]{1,0:T(8,128)(2,1)} %all-gather.5.cloned.1.call-done) | copy-start | bytes 15335428
  393.0 1.5 copy-start.10
  420.6 1.1 copy-start.7
  420.6 2.0 copy-start.8
  420.6 5.7 %slice-start = ((s8[5111808]{0:T(1024)(128)(4,1)}), s8[4194304]{0:T(1024)(128)(4,1)S(1)}, s32[]{:S(2)}) async-start(s8[5111808]{0:T(1024)(128)(4,1)} %bitcast.57), calls=%async_computation.10 | async-start | bytes 8388608
  422.6 3.8 slice-start.1
Sparse Core Ops, SparseCore 0:
  36.2 79.2 reduce-scatter.12
  118.9 79.1 reduce-scatter.14
  201.4 79.1 reduce-scatter.16
  282.9 46.0 all-gather.2
  331.1 55.6 all-gather.4
  396.1 29.9 reduce-scatter.10
where the time goes:
time: 447 us; the launch traced here: 446 us
  waiting for transfers between devices  317 us (71%)
  local copies, waits for them, and re-layouts  47.5 us (11%)
  matrix products  35.1 us (8%)
  blocking collectives  16.3 us (4%)
  other arithmetic  15.5 us (3%)
  between operations  14.3 us (3%)
    unnamed x9, waiting for transfers between devices  221 us
    all_gather x1, waiting for transfers between devices, body(): lax.all_gather(jnp.concatenate([gate_grad, up_grad], axis=1), 'row', axis...  51.6 us
    all_gather x1, waiting for transfers between devices, body(): hidden_all = lax.all_gather(hidden_mine, 'row', axis=0, tiled=True)  44.2 us
    unnamed x34, local copies, waits for them, and re-layouts  25.3 us
    mul x8, local copies, waits for them, and re-layouts, expand(): return (blocks * kept).reshape(rows_w, cols_w)  21 us
    all_gather x1, blocking collectives, body(): lax.all_gather(jnp.concatenate([tokens, out_grad], axis=1), 'col', axis=0...  16.3 us
    dot_general x3, matrix products, contract_last(): lax.dot_general(left, right, (((1,), (1,)), ((), ())), preferred_element_...  12.7 us
  transfers between devices with their start and end apart: 6, of which 5 were waited for; matrix products, arithmetic and copies ran while one was open for 15% of the time, Pallas kernels for 0%

commit v1 on v0

--- a/solution.py
+++ b/solution.py
@@ -49,7 +49,24 @@
     sigmoid_gate = jax.nn.sigmoid(gate_mine)
     silu_gate = gate_mine * sigmoid_gate
     hidden_mine = (silu_gate * up_mine).astype(jnp.bfloat16)
-    hidden_all = lax.all_gather(hidden_mine, "row", axis=0, tiled=True)
+    peers, index, rows = (lax.axis_size("row"), lax.axis_index("row"), hidden_mine.shape[0])
+    forward = [(i, (i + 1) % peers) for i in range(peers)]
+    left_2 = [(i, (i - 1) % peers) for i in range(peers)]
+    out = jnp.zeros(
+        (*hidden_mine.shape[:0], peers * rows, *hidden_mine.shape[0 + 1 :]), hidden_mine.dtype
+    )
+    out = lax.dynamic_update_slice_in_dim(out, hidden_mine, index * rows, axis=0)
+    from_left = from_right = hidden_mine
+    halfway = peers // 2
+    for turn in range(1, halfway + 1):
+        from_left = lax.ppermute(from_left, "row", forward)
+        out = lax.dynamic_update_slice_in_dim(out, from_left, (index - turn) % peers * rows, axis=0)
+        if turn < peers - halfway:
+            from_right = lax.ppermute(from_right, "row", left_2)
+            out = lax.dynamic_update_slice_in_dim(
+                out, from_right, (index + turn) % peers * rows, axis=0
+            )
+    hidden_all = out
     hidden_grad = lax.psum_scatter(
         contract_last(grad_all, w_down), "row", scatter_dimension=0, tiled=True
     )

time: 447 us -> 430 us (0.962)
  the two profiles are of different devices: /device:TPU:1 before, /device:TPU:0 now
where the time goes in v1:
time: 430 us
  waiting for transfers between devices  272 us (63%)
  local copies, waits for them, and re-layouts  46.4 us (11%)
  starting transfers between devices  38.9 us (9%)
  matrix products  31.5 us (7%)
  between operations  14.2 us (3%)
  blocking collectives  14 us (3%)
  other arithmetic  12.2 us (3%)
    unnamed x8, waiting for transfers between devices  228 us
    ppermute x7, starting transfers between devices, body(): from_right = lax.ppermute(from_right, 'row', left_2)  37.5 us
    ppermute x8, waiting for transfers between devices, body(): from_left = lax.ppermute(from_left, 'row', forward)  37.1 us
    unnamed x46, local copies, waits for them, and re-layouts  23.6 us
    mul x8, local copies, waits for them, and re-layouts, expand(): return (blocks * kept).reshape(rows_w, cols_w)  21.2 us
    all_gather x1, blocking collectives, body(): lax.all_gather(jnp.concatenate([tokens, out_grad], axis=1), 'col', axis=0...  14 us
    dot_general x3, matrix products, contract_last(): lax.dot_general(left, right, (((1,), (1,)), ((), ())), preferred_element_...  10.8 us
    dot_general x2, matrix products, contract_first(): lax.dot_general(left, right, (((0,), (0,)), ((), ())), preferred_element_...  9.45 us
  transfers between devices with their start and end apart: 20, of which 13 were waited for; matrix products, arithmetic and copies ran while one was open for 14% of the time, Pallas kernels for 0%

profile of v1, /device:TPU:0, one launch (start us, length us, event | category | flops | bytes accessed | tf_op | source)
XLA Modules:
  0.0 429.7 jit_solution(16458198252566617165)
XLA Ops:
  7.2 4.3 copy.26
  11.7 14.0 %all_gather.6 = bf16[384,1024]{1,0:T(8,128)(2,1)S(1)} all-gather(bf16[48,1024]{1,0:T(8,128)(2,1)S(1)} %pad_maximum_fusion.2), channel_id=1, replica_groups=mesh['row'=16,'col'=8] {'col'}, dimensions={0}, use_global_device_ids=true | all-gather | bytes 884736 | tf_op jit(solution)/shard_map/all_gather | solution.py:29
  28.4 3.9 fusion.10
  35.8 3.9 fusion.12
  39.8 4.3 %copy.28 = bf16[512,3328]{0,1:T(8,128)(2,1)S(1)} copy(bf16[512,3328]{1,0:T(8,128)(2,1)} %param.10) | data formatting | bytes 6815744 | tf_op args[2]
  47.0 3.9 fusion.11
  50.9 63.2 %reduce-scatter.13.cloned.1.call-done = f32[24,3328]{1,0:T(8,128)} async-done(((f32[384,3328]{1,0:T(8,128)}), f32[24,3328]{1,0:T(8,128)}) %reduce-scatter.13.cloned.1.call-update) | async-done | bytes 319504
  114.1 82.6 %reduce-scatter.17.cloned.1.call-done = f32[24,3328]{1,0:T(8,128)} async-done(((f32[384,3328]{1,0:T(8,128)}), f32[24,3328]{1,0:T(8,128)}) %reduce-scatter.17.cloned.1.call-update) | async-done | bytes 319504
  196.7 82.6 %reduce-scatter.15.cloned.1.call-done = f32[24,3328]{1,0:T(8,128)} async-done(((f32[384,3328]{1,0:T(8,128)}), f32[24,3328]{1,0:T(8,128)}) %reduce-scatter.15.cloned.1.call-update) | async-done | bytes 319504
  283.0 4.3 collective-permute-start.1
  290.5 5.3 %collective-permute-start.3 = (bf16[24,3328]{1,0:T(8,128)(2,1)S(1)}, bf16[24,3328]{1,0:T(8,128)(2,1)S(1)}, u32[]{:S(2)}, u32[]{:S(2)}) collective-permute-start(bf16[24,3328]{1,0:T(8,128)(2,1)S(1)} %collective-permute-done.1), channel_id=1, source_target_pairs={{0,120},{8,0},{16,8},{24,16},{32,24},{40,32},{48,40},{56,48},{64,5... | collective-permute-start | bytes 479240 | tf_op jit(solution)/shard_map/ppermute | solution.py:65
  295.9 6.1 %collective-permute-done.2 = bf16[24,3328]{1,0:T(8,128)(2,1)S(1)} collective-permute-done((bf16[24,3328]{1,0:T(8,128)(2,1)S(1)}, bf16[24,3328]{1,0:T(8,128)(2,1)S(1)}, u32[]{:S(2)}, u32[]{:S(2)}) %collective-permute-start.2) | collective-permute-done | bytes 159776 | tf_op jit(solution)/shard_map/ppermute | solution.py:62
  301.9 5.3 %collective-permute-start.5 = (bf16[24,3328]{1,0:T(8,128)(2,1)S(1)}, bf16[24,3328]{1,0:T(8,128)(2,1)S(1)}, u32[]{:S(2)}, u32[]{:S(2)}) collective-permute-start(bf16[24,3328]{1,0:T(8,128)(2,1)S(1)} %collective-permute-done.3), channel_id=1, source_target_pairs={{0,120},{8,0},{16,8},{24,16},{32,24},{40,32},{48,40},{56,48},{64,5... | collective-permute-start | bytes 479240 | tf_op jit(solution)/shard_map/ppermute | solution.py:65
  307.3 3.5 collective-permute-done.4
  310.8 5.6 %collective-permute-start.7 = (bf16[24,3328]{1,0:T(8,128)(2,1)S(1)}, bf16[24,3328]{1,0:T(8,128)(2,1)S(1)}, u32[]{:S(2)}, u32[]{:S(2)}) collective-permute-start(bf16[24,3328]{1,0:T(8,128)(2,1)S(1)} %collective-permute-done.5), channel_id=1, source_target_pairs={{0,120},{8,0},{16,8},{24,16},{32,24},{40,32},{48,40},{56,48},{64,5... | collective-permute-start | bytes 479240 | tf_op jit(solution)/shard_map/ppermute | solution.py:65
  316.5 4.4 %collective-permute-done.6 = bf16[24,3328]{1,0:T(8,128)(2,1)S(1)} collective-permute-done((bf16[24,3328]{1,0:T(8,128)(2,1)S(1)}, bf16[24,3328]{1,0:T(8,128)(2,1)S(1)}, u32[]{:S(2)}, u32[]{:S(2)}) %collective-permute-start.6) | collective-permute-done | bytes 159776 | tf_op jit(solution)/shard_map/ppermute | solution.py:62
  320.9 3.4 collective-permute-done.7
  324.3 5.8 %collective-permute-start.9 = (bf16[24,3328]{1,0:T(8,128)(2,1)S(1)}, bf16[24,3328]{1,0:T(8,128)(2,1)S(1)}, u32[]{:S(2)}, u32[]{:S(2)}) collective-permute-start(bf16[24,3328]{1,0:T(8,128)(2,1)S(1)} %collective-permute-done.7), channel_id=1, source_target_pairs={{0,120},{8,0},{16,8},{24,16},{32,24},{40,32},{48,40},{56,48},{64,5... | collective-permute-start | bytes 479240 | tf_op jit(solution)/shard_map/ppermute | solution.py:65
  330.2 4.2 collective-permute-done.8
  337.8 5.8 %collective-permute-start.11 = (bf16[24,3328]{1,0:T(8,128)(2,1)S(1)}, bf16[24,3328]{1,0:T(8,128)(2,1)S(1)}, u32[]{:S(2)}, u32[]{:S(2)}) collective-permute-start(bf16[24,3328]{1,0:T(8,128)(2,1)S(1)} %collective-permute-done.9), channel_id=1, source_target_pairs={{0,120},{8,0},{16,8},{24,16},{32,24},{40,32},{48,40},{56,48},{64,5... | collective-permute-start | bytes 479240 | tf_op jit(solution)/shard_map/ppermute | solution.py:65
  343.6 4.0 collective-permute-done.10
  347.6 5.3 %collective-permute-start.13 = (bf16[24,3328]{1,0:T(8,128)(2,1)S(1)}, bf16[24,3328]{1,0:T(8,128)(2,1)S(1)}, u32[]{:S(2)}, u32[]{:S(2)}) collective-permute-start(bf16[24,3328]{1,0:T(8,128)(2,1)S(1)} %collective-permute-done.11), channel_id=1, source_target_pairs={{0,120},{8,0},{16,8},{24,16},{32,24},{40,32},{48,40},{56,48},{64,5... | collective-permute-start | bytes 479240 | tf_op jit(solution)/shard_map/ppermute | solution.py:65
  356.3 8.5 %collective-permute-done.14 = bf16[24,3328]{1,0:T(8,128)(2,1)S(1)} collective-permute-done((bf16[24,3328]{1,0:T(8,128)(2,1)S(1)}, bf16[24,3328]{1,0:T(8,128)(2,1)S(1)}, u32[]{:S(2)}, u32[]{:S(2)}) %collective-permute-start.14) | collective-permute-done | bytes 159776 | tf_op jit(solution)/shard_map/ppermute | solution.py:62
  364.9 3.5 fusion.13
  368.5 5.4 %fusion.3 = f32[384,512]{1,0:T(8,128)S(1)} fusion(bf16[384,6656]{1,0:T(8,128)(2,1)} %all-gather.2.cloned.1.call-done, bf16[512,3328]{0,1:T(8,128)(2,1)} %copy-done.6, bf16[416,8,4,128]{3,2,1,0:T(4,128)(2,1)} %bitcast.56), kind=kOutput, calls=%fused_computation.11 | convolution fusion | flops 1310326784 | bytes 10158080 | tf_op jit(solution)/shard_map/dot_general | solution.py:16
  379.5 3.6 copy.53
  383.1 7.8 %copy.33 = f32[512,3328]{1,0:T(8,128)} copy(f32[512,3328]{0,1:T(8,128)} %bitcast.48) | data formatting | bytes 13631488 | tf_op jit(solution)/shard_map/mul | solution.py:12
  391.9 3.5 copy.54
  395.4 7.7 %copy.31 = f32[512,3328]{1,0:T(8,128)} copy(f32[512,3328]{0,1:T(8,128)} %bitcast.50) | data formatting | bytes 13631488 | tf_op jit(solution)/shard_map/mul | solution.py:12
  404.4 3.7 fusion
  408.1 5.7 %fusion.17 = f32[512,6656]{1,0:T(8,128)S(1)} fusion(bf16[384,6656]{1,0:T(8,128)(2,1)} %all-gather.2.cloned.1.call-done, bf16[384,1024]{1,0:T(8,128)(2,1)S(1)} %copy-done.11), kind=kOutput, calls=%fused_computation.29 | convolution fusion | flops 2617245696 | bytes 19136512 | tf_op jit(solution)/shard_map/dot_general | solution.py:22
  413.9 7.7 %fusion.1 = (bf16[512,3328]{1,0:T(8,128)(2,1)}, bf16[512,3328]{1,0:T(8,128)(2,1)}) fusion(f32[512,3328]{1,0:T(8,128)} %copy.33, f32[512,6656]{1,0:T(8,128)S(1)} %fusion.17, f32[512,3328]{1,0:T(8,128)} %copy.31), kind=kLoop, calls=%fused_computation.5 | loop fusion | flops 6815744 | bytes 34078720 | tf_op jit(solution)/shard_map/convert_element_type | solution.py:83
  (109 shorter events, 32.5 us)
Async XLA Ops:
  7.2 4.3 %copy-start.18 = (s32[4,26]{1,0:T(4,128)S(1)}, s32[4,26]{1,0:T(4,128)}, u32[]{:S(2)}) copy-start(s32[4,26]{1,0:T(4,128)} %param.12) | copy-start | bytes 1252
  7.2 4.5 %copy-start.16 = (bf16[48,512]{1,0:T(8,128)(2,1)S(1)}, bf16[48,512]{1,0:T(8,128)(2,1)}, u32[]{:S(2)}) copy-start(bf16[48,512]{1,0:T(8,128)(2,1)} %param.15) | copy-start | bytes 147460
  7.2 4.5 %copy-start.17 = (bf16[48,512]{1,0:T(8,128)(2,1)S(1)}, bf16[48,512]{1,0:T(8,128)(2,1)}, u32[]{:S(2)}) copy-start(bf16[48,512]{1,0:T(8,128)(2,1)} %param.8) | copy-start | bytes 147460
  7.2 106.9 %reduce-scatter.13.cloned.1.call-start = ((), (), s32[]{:S(2)}) async-start(), calls=%async_computation.6 | async-start | bytes 5431296
  11.5 20.8 %copy-start = (bf16[512,3328]{0,1:T(8,128)(2,1)}, bf16[512,3328]{0,1:T(8,128)(2,1)S(1)}, u32[]{:S(2)}) copy-start(bf16[512,3328]{0,1:T(8,128)(2,1)S(1)} %copy.26) | copy-start | bytes 10223620
  32.3 3.5 copy-start.9
  32.3 164.4 %reduce-scatter.17.cloned.1.call-start = ((), (), s32[]{:S(2)}) async-start(), calls=%async_computation.8 | async-start | bytes 5431296
  39.7 4.4 %copy-start.20 = (s32[4,26]{1,0:T(4,128)S(1)}, s32[4,26]{1,0:T(4,128)}, u32[]{:S(2)}) copy-start(s32[4,26]{1,0:T(4,128)} %param.13) | copy-start | bytes 1252
  39.7 239.6 %reduce-scatter.15.cloned.1.call-start = ((), (), s32[]{:S(2)}) async-start(), calls=%async_computation.7 | async-start | bytes 5431296
  44.1 6.8 %copy-start.6 = (bf16[512,3328]{0,1:T(8,128)(2,1)}, bf16[512,3328]{0,1:T(8,128)(2,1)S(1)}, u32[]{:S(2)}) copy-start(bf16[512,3328]{0,1:T(8,128)(2,1)S(1)} %copy.28) | copy-start | bytes 10223620
  50.9 317.5 %all-gather.2.cloned.1.call-start = ((), (), s32[]{:S(2)}) async-start(), calls=%async_computation.4 | async-start | bytes 5431296 | tf_op jit(solution)/shard_map/all_gather | solution.py:77
  114.1 167.6 %copy-start.14 = (f32[24,3328]{1,0:T(8,128)S(1)}, f32[24,3328]{1,0:T(8,128)}, u32[]{:S(2)}) copy-start(f32[24,3328]{1,0:T(8,128)} %reduce-scatter.13.cloned.1.call-done) | copy-start | bytes 958468
  281.5 140.1 %reduce-scatter.11.cloned.1.call-start = ((), (), s32[]{:S(2)}) async-start(), calls=%async_computation.5 | async-start | bytes 1769472 | tf_op jit(solution)/shard_map/reduce_scatter | solution.py:89
  281.8 8.7 %collective-permute-start = (bf16[24,3328]{1,0:T(8,128)(2,1)S(1)}, bf16[24,3328]{1,0:T(8,128)(2,1)S(1)}, u32[]{:S(2)}, u32[]{:S(2)}) collective-permute-start(bf16[24,3328]{1,0:T(8,128)(2,1)S(1)} %get-tuple-element.6), channel_id=1, source_target_pairs={{0,8},{8,16},{16,24},{24,32},{32,40},{40,48},{48,56},{56,64},{64,7... | collective-permute-start | bytes 479240 | tf_op jit(solution)/shard_map/ppermute | solution.py:62
  283.0 7.5 %collective-permute-start.1 = (bf16[24,3328]{1,0:T(8,128)(2,1)S(1)}, bf16[24,3328]{1,0:T(8,128)(2,1)S(1)}, u32[]{:S(2)}, u32[]{:S(2)}) collective-permute-start(bf16[24,3328]{1,0:T(8,128)(2,1)S(1)} %get-tuple-element.6), channel_id=1, source_target_pairs={{0,120},{8,0},{16,8},{24,16},{32,24},{40,32},{48,40},{56,48},{64,5... | collective-permute-start | bytes 479240 | tf_op jit(solution)/shard_map/ppermute | solution.py:65
  287.2 77.6 %copy-start.5 = (bf16[26,128,4,128]{3,2,1,0:T(4,128)(2,1)S(1)}, bf16[26,128,4,128]{3,2,1,0:T(4,128)(2,1)}, u32[]{:S(2)}) copy-start(bf16[26,128,4,128]{3,2,1,0:T(4,128)(2,1)} %copy-done.4) | copy-start | bytes 10223620
  290.5 11.5 %collective-permute-start.2 = (bf16[24,3328]{1,0:T(8,128)(2,1)S(1)}, bf16[24,3328]{1,0:T(8,128)(2,1)S(1)}, u32[]{:S(2)}, u32[]{:S(2)}) collective-permute-start(bf16[24,3328]{1,0:T(8,128)(2,1)S(1)} %collective-permute-done), channel_id=1, source_target_pairs={{0,8},{8,16},{16,24},{24,32},{32,40},{40,48},{48,56},{56,64},{64,7... | collective-permute-start | bytes 479240 | tf_op jit(solution)/shard_map/ppermute | solution.py:62
  290.5 11.5 %collective-permute-start.3 = (bf16[24,3328]{1,0:T(8,128)(2,1)S(1)}, bf16[24,3328]{1,0:T(8,128)(2,1)S(1)}, u32[]{:S(2)}, u32[]{:S(2)}) collective-permute-start(bf16[24,3328]{1,0:T(8,128)(2,1)S(1)} %collective-permute-done.1), channel_id=1, source_target_pairs={{0,120},{8,0},{16,8},{24,16},{32,24},{40,32},{48,40},{56,48},{64,5... | collective-permute-start | bytes 479240 | tf_op jit(solution)/shard_map/ppermute | solution.py:65
  301.9 8.9 %collective-permute-start.4 = (bf16[24,3328]{1,0:T(8,128)(2,1)S(1)}, bf16[24,3328]{1,0:T(8,128)(2,1)S(1)}, u32[]{:S(2)}, u32[]{:S(2)}) collective-permute-start(bf16[24,3328]{1,0:T(8,128)(2,1)S(1)} %collective-permute-done.2), channel_id=1, source_target_pairs={{0,8},{8,16},{16,24},{24,32},{32,40},{40,48},{48,56},{56,64},{64,7... | collective-permute-start | bytes 479240 | tf_op jit(solution)/shard_map/ppermute | solution.py:62
  301.9 8.9 %collective-permute-start.5 = (bf16[24,3328]{1,0:T(8,128)(2,1)S(1)}, bf16[24,3328]{1,0:T(8,128)(2,1)S(1)}, u32[]{:S(2)}, u32[]{:S(2)}) collective-permute-start(bf16[24,3328]{1,0:T(8,128)(2,1)S(1)} %collective-permute-done.3), channel_id=1, source_target_pairs={{0,120},{8,0},{16,8},{24,16},{32,24},{40,32},{48,40},{56,48},{64,5... | collective-permute-start | bytes 479240 | tf_op jit(solution)/shard_map/ppermute | solution.py:65
  310.8 10.1 %collective-permute-start.6 = (bf16[24,3328]{1,0:T(8,128)(2,1)S(1)}, bf16[24,3328]{1,0:T(8,128)(2,1)S(1)}, u32[]{:S(2)}, u32[]{:S(2)}) collective-permute-start(bf16[24,3328]{1,0:T(8,128)(2,1)S(1)} %collective-permute-done.4), channel_id=1, source_target_pairs={{0,8},{8,16},{16,24},{24,32},{32,40},{40,48},{48,56},{56,64},{64,7... | collective-permute-start | bytes 479240 | tf_op jit(solution)/shard_map/ppermute | solution.py:62
  310.8 13.5 %collective-permute-start.7 = (bf16[24,3328]{1,0:T(8,128)(2,1)S(1)}, bf16[24,3328]{1,0:T(8,128)(2,1)S(1)}, u32[]{:S(2)}, u32[]{:S(2)}) collective-permute-start(bf16[24,3328]{1,0:T(8,128)(2,1)S(1)} %collective-permute-done.5), channel_id=1, source_target_pairs={{0,120},{8,0},{16,8},{24,16},{32,24},{40,32},{48,40},{56,48},{64,5... | collective-permute-start | bytes 479240 | tf_op jit(solution)/shard_map/ppermute | solution.py:65
  320.9 13.5 %collective-permute-start.8 = (bf16[24,3328]{1,0:T(8,128)(2,1)S(1)}, bf16[24,3328]{1,0:T(8,128)(2,1)S(1)}, u32[]{:S(2)}, u32[]{:S(2)}) collective-permute-start(bf16[24,3328]{1,0:T(8,128)(2,1)S(1)} %collective-permute-done.6), channel_id=1, source_target_pairs={{0,8},{8,16},{16,24},{24,32},{32,40},{40,48},{48,56},{56,64},{64,7... | collective-permute-start | bytes 479240 | tf_op jit(solution)/shard_map/ppermute | solution.py:62
  324.3 13.5 %collective-permute-start.9 = (bf16[24,3328]{1,0:T(8,128)(2,1)S(1)}, bf16[24,3328]{1,0:T(8,128)(2,1)S(1)}, u32[]{:S(2)}, u32[]{:S(2)}) collective-permute-start(bf16[24,3328]{1,0:T(8,128)(2,1)S(1)} %collective-permute-done.7), channel_id=1, source_target_pairs={{0,120},{8,0},{16,8},{24,16},{32,24},{40,32},{48,40},{56,48},{64,5... | collective-permute-start | bytes 479240 | tf_op jit(solution)/shard_map/ppermute | solution.py:65
  334.4 13.2 %collective-permute-start.10 = (bf16[24,3328]{1,0:T(8,128)(2,1)S(1)}, bf16[24,3328]{1,0:T(8,128)(2,1)S(1)}, u32[]{:S(2)}, u32[]{:S(2)}) collective-permute-start(bf16[24,3328]{1,0:T(8,128)(2,1)S(1)} %collective-permute-done.8), channel_id=1, source_target_pairs={{0,8},{8,16},{16,24},{24,32},{32,40},{40,48},{48,56},{56,64},{64,7... | collective-permute-start | bytes 479240 | tf_op jit(solution)/shard_map/ppermute | solution.py:62
  337.8 9.8 %collective-permute-start.11 = (bf16[24,3328]{1,0:T(8,128)(2,1)S(1)}, bf16[24,3328]{1,0:T(8,128)(2,1)S(1)}, u32[]{:S(2)}, u32[]{:S(2)}) collective-permute-start(bf16[24,3328]{1,0:T(8,128)(2,1)S(1)} %collective-permute-done.9), channel_id=1, source_target_pairs={{0,120},{8,0},{16,8},{24,16},{32,24},{40,32},{48,40},{56,48},{64,5... | collective-permute-start | bytes 479240 | tf_op jit(solution)/shard_map/ppermute | solution.py:65
  347.6 8.6 %collective-permute-start.12 = (bf16[24,3328]{1,0:T(8,128)(2,1)S(1)}, bf16[24,3328]{1,0:T(8,128)(2,1)S(1)}, u32[]{:S(2)}, u32[]{:S(2)}) collective-permute-start(bf16[24,3328]{1,0:T(8,128)(2,1)S(1)} %collective-permute-done.10), channel_id=1, source_target_pairs={{0,8},{8,16},{16,24},{24,32},{32,40},{40,48},{48,56},{56,64},{64,7... | collective-permute-start | bytes 479240 | tf_op jit(solution)/shard_map/ppermute | solution.py:62
  347.6 8.6 %collective-permute-start.13 = (bf16[24,3328]{1,0:T(8,128)(2,1)S(1)}, bf16[24,3328]{1,0:T(8,128)(2,1)S(1)}, u32[]{:S(2)}, u32[]{:S(2)}) collective-permute-start(bf16[24,3328]{1,0:T(8,128)(2,1)S(1)} %collective-permute-done.11), channel_id=1, source_target_pairs={{0,120},{8,0},{16,8},{24,16},{32,24},{40,32},{48,40},{56,48},{64,5... | collective-permute-start | bytes 479240 | tf_op jit(solution)/shard_map/ppermute | solution.py:65
  356.2 8.6 %collective-permute-start.14 = (bf16[24,3328]{1,0:T(8,128)(2,1)S(1)}, bf16[24,3328]{1,0:T(8,128)(2,1)S(1)}, u32[]{:S(2)}, u32[]{:S(2)}) collective-permute-start(bf16[24,3328]{1,0:T(8,128)(2,1)S(1)} %collective-permute-done.12), channel_id=1, source_target_pairs={{0,8},{8,16},{16,24},{24,32},{32,40},{40,48},{48,56},{56,64},{64,7... | collective-permute-start | bytes 479240 | tf_op jit(solution)/shard_map/ppermute | solution.py:62
  368.4 5.4 %copy-start.1 = (bf16[512,3328]{0,1:T(8,128)(2,1)S(1)}, bf16[512,3328]{0,1:T(8,128)(2,1)}, u32[]{:S(2)}) copy-start(bf16[512,3328]{0,1:T(8,128)(2,1)} %copy-done) | copy-start | bytes 10223620
  368.4 5.7 %copy-start.3 = (bf16[4,128,26,128]{1,0,3,2:T(4,128)(2,1)S(1)}, bf16[4,128,26,128]{1,0,3,2:T(4,128)(2,1)}, u32[]{:S(2)}) copy-start(bf16[4,128,26,128]{1,0,3,2:T(4,128)(2,1)} %copy-done.2) | copy-start | bytes 10223620
  368.4 7.2 %copy-start.12 = (bf16[384,6656]{1,0:T(8,128)(2,1)S(1)}, bf16[384,6656]{1,0:T(8,128)(2,1)}, u32[]{:S(2)}) copy-start(bf16[384,6656]{1,0:T(8,128)(2,1)} %all-gather.2.cloned.1.call-done) | copy-start | bytes 15335428
  (9 other events, 15.9 us)
Sparse Core Ops, SparseCore 0:
  32.4 81.6 reduce-scatter.12
  117.5 79.1 reduce-scatter.16
  200.1 79.2 reduce-scatter.14
  281.6 67.3 all-gather.1
  378.6 29.1 reduce-scatter.10
